TPU v7x, 512 devices: a whole 4x8x8 slice. The times are simulated.
512 devices in a mesh: dp: 64 (over x, z, core), refl: 8 (over y).
Axes of the slice: x: 4, y: 8, z: 8, core: 2. Of those that a mesh axis runs over, the one named last changes fastest.
Arguments:
- intensities: bfloat16 [2048, 16384], P('dp', 'refl'), may hold values from -12 to 12
- observed: int32 [2048, 16384], P('dp', 'refl'), may hold values 0 or 1
- qweights: bfloat16 [2048, 16384], P('dp', 'refl'), may hold values from 0.25 to 4
- ops: int32 [4, 16384], P(None, 'refl'), may hold values from 0 to 16383, as said below
- pick: int32 [64, 64], P(None, 'dp'), may hold values from 0 to 7
Outputs:
- corr: float32 [4, 2048, 256], P(None, ('dp', 'refl'))
- returned: float32 [4, 64, 64, 4, 32], P(None, 'dp', None, None, 'refl')
Inputs may be any that keep to these rules, and one draw needn't show every extreme that they name: Each row of ops is a permutation of the reflections that maps every aligned block of 2048 reflections onto itself.
All inputs are finite; a program needn't handle non-finite values. No bound on the sum of `observed` on one device may be relied on, other than what follows from the above.
Results may differ from a plain program's by a relative error of at most 0.0084.
Values may be sent and summed in bfloat16 or wider, within the bound.
A program may use at most 64 MiB of HBM per device.

v0:
```python
import jax
import jax.numpy as jnp
from jax import lax
from jax.sharding import PartitionSpec as P

SUB = 4
NOPS = 4


def gram(left, right):
    return lax.dot_general(
        left, right, (((1,), (1,)), ((), ())), preferred_element_type=jnp.float32
    )


def collect(stacked_own, blk, part_w, part_wy, part_wyy):
    first = gram(stacked_own, part_w).reshape(3, blk, -1)
    second = gram(stacked_own[: 2 * blk], part_wy).reshape(2, blk, -1)
    third = gram(stacked_own[:blk], part_wyy)[None]
    return jnp.concatenate([first, second, third], 0)


def pearson(share):
    total_w, sum_x, sum_xx = (share[:, 0], share[:, 1], share[:, 2])
    sum_y, sum_xy, sum_yy = (share[:, 3], share[:, 4], share[:, 5])
    numer = total_w * sum_xy - sum_x * sum_y
    var_x = jnp.maximum(total_w * sum_xx - sum_x * sum_x, 0.05 * total_w * sum_xx)
    var_y = jnp.maximum(total_w * sum_yy - sum_y * sum_y, 0.05 * total_w * sum_yy)
    return numer / jnp.sqrt(var_x * var_y)


def shards(intensities, observed, qweights, ops, pick):
    blk = intensities.shape[0]
    width = intensities.shape[1]
    groups = lax.axis_size("dp")
    shares = lax.axis_size("refl")
    weights = observed.astype(jnp.float32) * qweights.astype(jnp.float32)
    values = intensities.astype(jnp.float32)
    own_w = weights.astype(jnp.bfloat16)
    own_wx = (weights * values).astype(jnp.bfloat16)
    own_wxx = (weights * values * values).astype(jnp.bfloat16)
    stacked_own = jnp.concatenate([own_w, own_wx, own_wxx], 0)
    local_ops = ops - lax.axis_index("refl") * width
    request = pick[:, 0][:, None] * SUB + jnp.arange(SUB, dtype=jnp.int32)[None, :]
    send_x = intensities[request]
    send_w = own_w[request]
    got_x = lax.all_to_all(send_x, "dp", split_axis=0, concat_axis=0, tiled=True)
    got_w = lax.all_to_all(send_w, "dp", split_axis=0, concat_axis=0, tiled=True)
    count = got_x.shape[1]
    flat_x = got_x.reshape(-1, width)
    flat_w = got_w.reshape(-1, width)
    per_op = []
    for k in range(NOPS):
        perm = local_ops[k]
        moved_w = jnp.take(flat_w, perm, axis=1)
        wide_w = moved_w.astype(jnp.float32)
        wide_x = jnp.take(flat_x, perm, axis=1).astype(jnp.float32)
        moved_wy = (wide_w * wide_x).astype(jnp.bfloat16)
        moved_wyy = (wide_w * wide_x * wide_x).astype(jnp.bfloat16)
        per_op.append(collect(stacked_own, blk, moved_w, moved_wy, moved_wyy))
    stats = jnp.stack(per_op, 0)
    stats = stats.reshape(NOPS, 6, blk, groups, count)
    flat_stats = stats.reshape(NOPS, 6, blk, -1)
    rows = blk // shares
    totals = lax.psum(flat_stats, "refl")
    share = lax.dynamic_slice_in_dim(totals, lax.axis_index("refl") * rows, rows, 2)
    corr = pearson(share)
    outgoing = jnp.transpose(corr.reshape(NOPS, rows, groups, SUB), (0, 2, 3, 1))[:, :, None]
    returned = lax.all_to_all(outgoing, "dp", split_axis=1, concat_axis=2, tiled=True)
    return (corr, returned)


def solution(mesh):
    return jax.shard_map(
        shards,
        mesh=mesh,
        in_specs=(
            P("dp", "refl"),
            P("dp", "refl"),
            P("dp", "refl"),
            P(None, "refl"),
            P(None, "dp"),
        ),
        out_specs=(P(None, ("dp", "refl"), None), P(None, "dp", None, None, "refl")),
        check_vma=False,
    )
```

profile of v0, /device:TPU:1, one launch (start us, length us, event | category | flops | bytes accessed | tf_op | source)
XLA Modules:
  0.0 299.3 jit_solution(15204998179728151762)
XLA Ops:
  7.2 0.7 multiply_bitcast_fusion.1
  7.8 0.1 compare_select_fusion
  7.9 0.1 reshape.173
  8.0 3.3 %gather_fusion.1 = bf16[256,2048]{1,0:T(8,128)(2,1)S(1)} fusion(bf16[32,2048]{1,0:T(8,128)(2,1)} %param.7, s32[1024]{0:T(1024)S(1)} %pad_clamp_fusion), kind=kCustom, calls=%fused_computation.9 | custom fusion | bytes 2098176 | tf_op jit(solution)/shard_map/gather | solution.py:45
  11.3 1.2 reshape.180
  12.5 15.0 %all-to-all-start.1 = ((bf16[64,4,2048]{2,1,0:T(4,128)(2,1)}), bf16[64,4,2048]{2,1,0:T(4,128)(2,1)S(1)}, u32[]{:S(2)}, u32[]{:S(2)}) async-start(bf16[64,4,2048]{2,1,0:T(4,128)(2,1)} %reshape.180), calls=%async_computation.1 | async-start | bytes 2097152 | tf_op jit(solution)/shard_map/all_to_all | solution.py:47
  27.5 0.1 fusion.44
  27.6 1.4 gather_fusion
  29.0 0.0 copy-start.16
  29.0 1.2 reshape.172
  30.2 25.8 %all-to-all-done.1 = bf16[64,4,2048]{2,1,0:T(4,128)(2,1)S(1)} async-done(((bf16[64,4,2048]{2,1,0:T(4,128)(2,1)}), bf16[64,4,2048]{2,1,0:T(4,128)(2,1)S(1)}, u32[]{:S(2)}, u32[]{:S(2)}) %all-to-all-start.1) | async-done | bytes 1048608 | tf_op jit(solution)/shard_map/all_to_all | solution.py:47
  56.0 6.2 %all-to-all-start = ((bf16[64,4,2048]{2,1,0:T(4,128)(2,1)}), bf16[64,4,2048]{2,1,0:T(4,128)(2,1)S(1)}, u32[]{:S(2)}, u32[]{:S(2)}) async-start(bf16[64,4,2048]{2,1,0:T(4,128)(2,1)} %reshape.172), calls=%async_computation | async-start | bytes 2097152 | tf_op jit(solution)/shard_map/all_to_all | solution.py:48
  62.2 0.2 all-reduce.2.cloned.1.call-start
  62.5 0.6 compare_and_fusion.1
  63.1 0.6 compare_and_fusion
  63.7 0.6 compare_and_fusion.3
  64.3 0.6 compare_and_fusion.2
  64.9 0.6 fusion.54
  65.5 0.6 fusion.55
  66.1 0.3 reshape.99
  66.4 0.5 copy.19
  66.9 23.8 %all-to-all-done = bf16[64,4,2048]{2,1,0:T(4,128)(2,1)S(1)} async-done(((bf16[64,4,2048]{2,1,0:T(4,128)(2,1)}), bf16[64,4,2048]{2,1,0:T(4,128)(2,1)S(1)}, u32[]{:S(2)}, u32[]{:S(2)}) %all-to-all-start) | async-done | bytes 1048608 | tf_op jit(solution)/shard_map/all_to_all | solution.py:48
  90.8 0.3 reshape.97
  91.0 0.5 copy.18
  91.6 9.8 %gather_fusion.7 = bf16[2048,256]{1,0:T(8,128)(2,1)} fusion(bf16[256,2048]{0,1:T(8,128)(2,1)S(1)} %copy.19, s32[2048]{0:T(1024)} %fusion.54), kind=kCustom, calls=%fused_computation.5.clone | custom fusion | bytes 2105344 | tf_op jit(solution)/shard_map/jit(_take)/gather | solution.py:57
  101.3 8.5 %gather_fusion.6 = bf16[2048,256]{1,0:T(8,128)(2,1)S(1)} fusion(bf16[256,2048]{0,1:T(8,128)(2,1)S(1)} %copy.18, s32[2048]{0:T(1024)} %fusion.54), kind=kCustom, calls=%fused_computation.4.clone | custom fusion | bytes 2105344 | tf_op jit(solution)/shard_map/jit(_take)/gather | solution.py:55
  109.8 9.7 %gather_fusion.9 = bf16[2048,256]{1,0:T(8,128)(2,1)} fusion(bf16[256,2048]{0,1:T(8,128)(2,1)S(1)} %copy.19, s32[2048]{0:T(1024)} %fusion.55), kind=kCustom, calls=%fused_computation.7.clone | custom fusion | bytes 2105344 | tf_op jit(solution)/shard_map/jit(_take)/gather | solution.py:57
  119.5 9.8 %gather_fusion.8 = bf16[2048,256]{1,0:T(8,128)(2,1)} fusion(bf16[256,2048]{0,1:T(8,128)(2,1)S(1)} %copy.18, s32[2048]{0:T(1024)} %fusion.55), kind=kCustom, calls=%fused_computation.6.clone | custom fusion | bytes 2105344 | tf_op jit(solution)/shard_map/jit(_take)/gather | solution.py:55
  129.3 2.6 convolution_bitcast_fusion.1
  132.0 1.2 fusion.12
  133.2 0.3 copy-done.3
  133.5 1.3 convolution_bitcast_fusion
  134.8 1.2 fusion.14
  136.0 1.2 fusion.30
  137.2 1.2 fusion.24
  138.3 9.0 %gather_fusion.3 = bf16[2048,256]{1,0:T(8,128)(2,1)} fusion(bf16[256,2048]{0,1:T(8,128)(2,1)S(1)} %copy.19, s32[2048]{0:T(1024)S(1)} %fusion.52), kind=kCustom, calls=%fused_computation.1.clone | custom fusion | bytes 2105344 | tf_op jit(solution)/shard_map/jit(_take)/gather | solution.py:57
  147.3 7.5 %gather_fusion.2 = bf16[2048,256]{1,0:T(8,128)(2,1)S(1)} fusion(bf16[256,2048]{0,1:T(8,128)(2,1)S(1)} %copy.18, s32[2048]{0:T(1024)S(1)} %fusion.52), kind=kCustom, calls=%fused_computation.clone | custom fusion | bytes 2105344 | tf_op jit(solution)/shard_map/jit(_take)/gather | solution.py:55
  154.9 2.6 convolution_bitcast_fusion.3
  157.5 1.3 fusion.8
  158.8 1.2 fusion.42
  159.9 7.5 %gather_fusion.5 = bf16[2048,256]{1,0:T(8,128)(2,1)S(1)} fusion(bf16[256,2048]{0,1:T(8,128)(2,1)S(1)} %copy.19, s32[2048]{0:T(1024)S(1)} %fusion.53), kind=kCustom, calls=%fused_computation.3.clone | custom fusion | bytes 2105344 | tf_op jit(solution)/shard_map/jit(_take)/gather | solution.py:57
  167.4 7.7 %gather_fusion.4 = bf16[2048,256]{1,0:T(8,128)(2,1)S(1)} fusion(bf16[256,2048]{0,1:T(8,128)(2,1)S(1)} %copy.18, s32[2048]{0:T(1024)S(1)} %fusion.53), kind=kCustom, calls=%fused_computation.2.clone | custom fusion | bytes 2105344 | tf_op jit(solution)/shard_map/jit(_take)/gather | solution.py:55
  175.2 0.7 convolution_bitcast_fusion.2
  175.8 0.6 fusion.10
  176.6 0.5 fusion.36
  177.1 0.3 copy-done.7
  177.4 0.0 copy-done.8
  177.4 0.0 copy-done.11
  177.5 0.1 copy-done.9
  177.6 1.0 pad_maximum_fusion
  178.6 0.0 all-reduce.2.cloned.1.call-update
  178.6 72.0 %all-reduce.2.cloned.1.call-done = f32[4,6,32,256]{3,2,0,1:T(8,128)} async-done(((f32[4,6,32,256]{3,2,0,1:T(8,128)}), f32[4,6,32,256]{3,2,0,1:T(8,128)}) %all-reduce.2.cloned.1.call-update) | async-done | bytes 786448 | tf_op jit(solution)/shard_map/psum | solution.py:65
  250.7 1.5 fusion.50
  252.1 0.5 squeeze.45
  252.7 0.5 mul.158
  253.2 0.5 squeeze.42
  253.8 0.5 squeeze.44
  254.3 0.5 mul.154
  254.9 0.5 mul.152
  255.4 1.4 squeeze.43
  256.8 1.4 multiply_bitcast_fusion
  258.2 0.3 copy.26
  258.6 33.0 %all_to_all.22 = f32[4,64,1,4,4]{3,4,0,2,1:T(4,128)S(1)} all-to-all(f32[4,64,1,4,4]{3,4,0,2,1:T(4,128)S(1)} %copy.26), channel_id=1, replica_groups=mesh['dp'=64,'refl'=8] {'dp'}, dimensions={1} | all-to-all | bytes 32768 | tf_op jit(solution)/shard_map/all_to_all | solution.py:69
  291.5 0.9 copy.27
  (43 shorter events, 0.2 us)
Async XLA Ops:
  12.5 15.0 %copy-start = (bf16[32,2048]{1,0:T(8,128)(2,1)S(1)}, bf16[32,2048]{1,0:T(8,128)(2,1)}, u32[]{:S(2)}) copy-start(bf16[32,2048]{1,0:T(8,128)(2,1)} %param.7) | copy-start | bytes 393220
  12.5 15.0 %copy-start.5 = (s32[32,2048]{1,0:T(8,128)S(1)}, s32[32,2048]{1,0:T(8,128)}, u32[]{:S(2)}) copy-start(s32[32,2048]{1,0:T(8,128)} %param.8) | copy-start | bytes 786436
  12.5 15.0 %copy-start.6 = (bf16[32,2048]{1,0:T(8,128)(2,1)S(1)}, bf16[32,2048]{1,0:T(8,128)(2,1)}, u32[]{:S(2)}) copy-start(bf16[32,2048]{1,0:T(8,128)(2,1)} %param.9) | copy-start | bytes 393220
  12.5 43.5 %all-to-all-start.1 = ((bf16[64,4,2048]{2,1,0:T(4,128)(2,1)}), bf16[64,4,2048]{2,1,0:T(4,128)(2,1)S(1)}, u32[]{:S(2)}, u32[]{:S(2)}) async-start(bf16[64,4,2048]{2,1,0:T(4,128)(2,1)} %reshape.180), calls=%async_computation.1 | async-start | bytes 2097152 | tf_op jit(solution)/shard_map/all_to_all | solution.py:47
  29.0 1.2 copy-start.16
  56.0 34.7 %all-to-all-start = ((bf16[64,4,2048]{2,1,0:T(4,128)(2,1)}), bf16[64,4,2048]{2,1,0:T(4,128)(2,1)S(1)}, u32[]{:S(2)}, u32[]{:S(2)}) async-start(bf16[64,4,2048]{2,1,0:T(4,128)(2,1)} %reshape.172), calls=%async_computation | async-start | bytes 2097152 | tf_op jit(solution)/shard_map/all_to_all | solution.py:48
  62.2 188.4 %all-reduce.2.cloned.1.call-start = ((), (), s32[]{:S(2)}) async-start(), calls=%async_computation.3 | async-start | bytes 1572864 | tf_op jit(solution)/shard_map/psum | solution.py:65
  129.3 2.6 copy-start.2
  129.3 2.6 copy-start.20
  132.0 1.3 copy-start.1
  132.0 1.5 copy-start.3
  132.0 1.5 copy-start.19
  154.8 2.7 copy-start.4
  154.9 2.7 copy-start.18
  167.4 7.7 %copy-start.17 = (pred[2048]{0:T(1024)(128)(4,1)S(1)}, pred[2048]{0:T(1024)(128)(4,1)}, u32[]{:S(2)}) copy-start(pred[2048]{0:T(1024)(128)(4,1)} %compare_and_fusion.2) | copy-start | bytes 6148
  176.5 0.9 copy-start.7
  176.5 0.9 copy-start.8
  176.5 0.9 copy-start.10
  176.5 0.9 copy-start.11
  176.5 0.9 copy-start.13
  176.5 0.9 copy-start.14
  176.5 1.0 copy-start.9
  176.6 1.0 copy-start.12
  176.6 1.0 copy-start.15
Sparse Core Ops, SparseCore 0:
  178.8 71.8 all-reduce.1
where the time goes:
time: 301 us; the launch traced here: 299 us
  waiting for transfers between devices  122 us (41%)
  local copies, waits for them, and re-layouts  84.9 us (28%)
  blocking collectives  33 us (11%)
  starting transfers between devices  21.4 us (7%)
  matrix products  15.6 us (5%)
  between operations  14.4 us (5%)
  other arithmetic  8.37 us (3%)
    psum x1, waiting for transfers between devices, shards(): totals = lax.psum(flat_stats, 'refl')  72 us
    gather x4, local copies, waits for them, and re-layouts, shards(): wide_x = jnp.take(flat_x, perm, axis=1).astype(jnp.float32)  36 us
    gather x4, local copies, waits for them, and re-layouts, shards(): moved_w = jnp.take(flat_w, perm, axis=1)  33.5 us
    all_to_all x1, blocking collectives, shards(): lax.all_to_all(outgoing, 'dp', split_axis=1, concat_axis=2, tiled=True)  33 us
    all_to_all x1, waiting for transfers between devices, shards(): lax.all_to_all(send_x, 'dp', split_axis=0, concat_axis=0, tiled=True)  25.8 us
    all_to_all x1, waiting for transfers between devices, shards(): lax.all_to_all(send_w, 'dp', split_axis=0, concat_axis=0, tiled=True)  23.8 us
    dot_general x12, matrix products, gram(): lax.dot_general(left, right, (((1,), (1,)), ((), ())), preferred_element_...  15.6 us
    all_to_all x1, starting transfers between devices, shards(): lax.all_to_all(send_x, 'dp', split_axis=0, concat_axis=0, tiled=True)  15 us
  transfers between devices with their start and end apart: 3, of which 3 were waited for; matrix products, arithmetic and copies ran while one was open for 2% of the time, Pallas kernels for 0%

commit v1 on v0

--- a/solution.py
+++ b/solution.py
@@ -5,6 +5,14 @@
 
 SUB = 4
 NOPS = 4
+
+
+def add_in_pairs(x, axis):
+    count, total = (lax.axis_size(axis), x)
+    for far in [1 << k for k in range(count.bit_length() - 1)]:
+        pairs = [(i, i ^ far) for i in range(count)]
+        total = total + lax.ppermute(total, axis, pairs)
+    return total
 
 
 def gram(left, right):
@@ -62,7 +70,7 @@
     stats = stats.reshape(NOPS, 6, blk, groups, count)
     flat_stats = stats.reshape(NOPS, 6, blk, -1)
     rows = blk // shares
-    totals = lax.psum(flat_stats, "refl")
+    totals = add_in_pairs(flat_stats, "refl")
     share = lax.dynamic_slice_in_dim(totals, lax.axis_index("refl") * rows, rows, 2)
     corr = pearson(share)
     outgoing = jnp.transpose(corr.reshape(NOPS, rows, groups, SUB), (0, 2, 3, 1))[:, :, None]

time: 301 us -> 307 us (1.020)
  starting transfers between devices: 21.4 us -> 37.1 us
  waiting for transfers between devices: 122 us -> 136 us
  between operations: 14.4 us -> 1.09 us
  blocking collectives: 33 us -> 24.5 us
    ppermute x0 -> x3, waiting for transfers between devices: none -> 85.7 us  [add_in_pairs(): total = total + lax.ppermute(total, axis, pairs)]
    psum x1 -> x0, waiting for transfers between devices: 72 us -> none  [shards(): totals = lax.psum(flat_stats, 'refl')]
    ppermute x0 -> x3, starting transfers between devices: none -> 16 us  [add_in_pairs(): total = total + lax.ppermute(total, axis, pairs)]
    all_to_all x1, blocking collectives: 33 us -> 24.5 us  [shards(): lax.all_to_all(outgoing, 'dp', split_axis=1, concat_axis=2, tiled=True)]
  transfers between devices with their start and end apart: 3 -> 5, of which waited for: 3 -> 5; matrix products, arithmetic and copies ran while one was open for 2% -> 2% of each run, Pallas kernels for 0% -> 0%
where the time goes in v1:
time: 307 us; the launch traced here: 305 us
  waiting for transfers between devices  136 us (44%)
  local copies, waits for them, and re-layouts  84.6 us (28%)
  starting transfers between devices  37.1 us (12%)
  blocking collectives  24.5 us (8%)
  matrix products  15.5 us (5%)
  other arithmetic  6.96 us (2%)
    ppermute x3, waiting for transfers between devices, add_in_pairs(): total = total + lax.ppermute(total, axis, pairs)  85.7 us
    gather x4, local copies, waits for them, and re-layouts, shards(): wide_x = jnp.take(flat_x, perm, axis=1).astype(jnp.float32)  35.9 us
    gather x4, local copies, waits for them, and re-layouts, shards(): moved_w = jnp.take(flat_w, perm, axis=1)  33.2 us
    all_to_all x1, waiting for transfers between devices, shards(): lax.all_to_all(send_x, 'dp', split_axis=0, concat_axis=0, tiled=True)  25.8 us
    all_to_all x1, blocking collectives, shards(): lax.all_to_all(outgoing, 'dp', split_axis=1, concat_axis=2, tiled=True)  24.5 us
    all_to_all x1, waiting for transfers between devices, shards(): lax.all_to_all(send_w, 'dp', split_axis=0, concat_axis=0, tiled=True)  24.1 us
    ppermute x3, starting transfers between devices, add_in_pairs(): total = total + lax.ppermute(total, axis, pairs)  16 us
    dot_general x12, matrix products, gram(): lax.dot_general(left, right, (((1,), (1,)), ((), ())), preferred_element_...  15.5 us
  transfers between devices with their start and end apart: 5, of which 5 were waited for; matrix products, arithmetic and copies ran while one was open for 2% of the time, Pallas kernels for 0%

profile of v1, /device:TPU:1, one launch (start us, length us, event | category | flops | bytes accessed | tf_op | source)
XLA Modules:
  0.0 305.4 jit_solution(13412617419979126282)
XLA Ops:
  0.6 0.7 multiply_bitcast_fusion.1
  1.3 0.1 compare_select_fusion
  1.4 0.1 reshape.173
  1.5 3.3 %gather_fusion.1 = bf16[256,2048]{1,0:T(8,128)(2,1)S(1)} fusion(bf16[32,2048]{1,0:T(8,128)(2,1)} %param.7, s32[1024]{0:T(1024)S(1)} %pad_clamp_fusion), kind=kCustom, calls=%fused_computation.9 | custom fusion | bytes 2098176 | tf_op jit(solution)/shard_map/gather | solution.py:53
  4.8 1.2 reshape.180
  6.0 15.0 %all-to-all-start.1 = ((bf16[64,4,2048]{2,1,0:T(4,128)(2,1)}), bf16[64,4,2048]{2,1,0:T(4,128)(2,1)S(1)}, u32[]{:S(2)}, u32[]{:S(2)}) async-start(bf16[64,4,2048]{2,1,0:T(4,128)(2,1)} %reshape.180), calls=%async_computation.1 | async-start | bytes 2097152 | tf_op jit(solution)/shard_map/all_to_all | solution.py:55
  21.1 1.4 gather_fusion
  22.5 1.2 reshape.172
  23.7 25.8 %all-to-all-done.1 = bf16[64,4,2048]{2,1,0:T(4,128)(2,1)S(1)} async-done(((bf16[64,4,2048]{2,1,0:T(4,128)(2,1)}), bf16[64,4,2048]{2,1,0:T(4,128)(2,1)S(1)}, u32[]{:S(2)}, u32[]{:S(2)}) %all-to-all-start.1) | async-done | bytes 1048608 | tf_op jit(solution)/shard_map/all_to_all | solution.py:55
  49.5 6.2 %all-to-all-start = ((bf16[64,4,2048]{2,1,0:T(4,128)(2,1)}), bf16[64,4,2048]{2,1,0:T(4,128)(2,1)S(1)}, u32[]{:S(2)}, u32[]{:S(2)}) async-start(bf16[64,4,2048]{2,1,0:T(4,128)(2,1)} %reshape.172), calls=%async_computation | async-start | bytes 2097152 | tf_op jit(solution)/shard_map/all_to_all | solution.py:56
  55.7 0.6 compare_and_fusion.1
  56.3 0.6 compare_and_fusion
  56.9 0.6 compare_and_fusion.3
  57.5 0.6 compare_and_fusion.2
  58.1 0.6 fusion.54
  58.7 0.6 fusion.55
  59.3 0.3 reshape.99
  59.6 0.5 copy.19
  60.1 24.1 %all-to-all-done = bf16[64,4,2048]{2,1,0:T(4,128)(2,1)S(1)} async-done(((bf16[64,4,2048]{2,1,0:T(4,128)(2,1)}), bf16[64,4,2048]{2,1,0:T(4,128)(2,1)S(1)}, u32[]{:S(2)}, u32[]{:S(2)}) %all-to-all-start) | async-done | bytes 1048608 | tf_op jit(solution)/shard_map/all_to_all | solution.py:56
  84.2 0.3 reshape.97
  84.5 0.5 copy.18
  85.0 9.7 %gather_fusion.7 = bf16[2048,256]{1,0:T(8,128)(2,1)} fusion(bf16[256,2048]{0,1:T(8,128)(2,1)S(1)} %copy.19, s32[2048]{0:T(1024)} %fusion.54), kind=kCustom, calls=%fused_computation.5.clone | custom fusion | bytes 2105344 | tf_op jit(solution)/shard_map/jit(_take)/gather | solution.py:65
  94.7 8.5 %gather_fusion.6 = bf16[2048,256]{1,0:T(8,128)(2,1)S(1)} fusion(bf16[256,2048]{0,1:T(8,128)(2,1)S(1)} %copy.18, s32[2048]{0:T(1024)} %fusion.54), kind=kCustom, calls=%fused_computation.4.clone | custom fusion | bytes 2105344 | tf_op jit(solution)/shard_map/jit(_take)/gather | solution.py:63
  103.2 9.7 %gather_fusion.9 = bf16[2048,256]{1,0:T(8,128)(2,1)} fusion(bf16[256,2048]{0,1:T(8,128)(2,1)S(1)} %copy.19, s32[2048]{0:T(1024)} %fusion.55), kind=kCustom, calls=%fused_computation.7.clone | custom fusion | bytes 2105344 | tf_op jit(solution)/shard_map/jit(_take)/gather | solution.py:65
  113.0 9.7 %gather_fusion.8 = bf16[2048,256]{1,0:T(8,128)(2,1)} fusion(bf16[256,2048]{0,1:T(8,128)(2,1)S(1)} %copy.18, s32[2048]{0:T(1024)} %fusion.55), kind=kCustom, calls=%fused_computation.6.clone | custom fusion | bytes 2105344 | tf_op jit(solution)/shard_map/jit(_take)/gather | solution.py:63
  122.7 2.6 convolution_bitcast_fusion.1
  125.3 1.2 fusion.12
  126.6 0.3 copy-done.3
  126.9 1.3 convolution_bitcast_fusion
  128.1 1.2 fusion.14
  129.4 1.2 fusion.30
  130.5 1.1 fusion.24
  131.7 9.0 %gather_fusion.3 = bf16[2048,256]{1,0:T(8,128)(2,1)} fusion(bf16[256,2048]{0,1:T(8,128)(2,1)S(1)} %copy.19, s32[2048]{0:T(1024)S(1)} %fusion.52), kind=kCustom, calls=%fused_computation.1.clone | custom fusion | bytes 2105344 | tf_op jit(solution)/shard_map/jit(_take)/gather | solution.py:65
  140.7 7.5 %gather_fusion.2 = bf16[2048,256]{1,0:T(8,128)(2,1)S(1)} fusion(bf16[256,2048]{0,1:T(8,128)(2,1)S(1)} %copy.18, s32[2048]{0:T(1024)S(1)} %fusion.52), kind=kCustom, calls=%fused_computation.clone | custom fusion | bytes 2105344 | tf_op jit(solution)/shard_map/jit(_take)/gather | solution.py:63
  148.2 2.6 convolution_bitcast_fusion.3
  150.8 1.2 fusion.8
  152.1 1.2 fusion.42
  153.2 7.5 %gather_fusion.5 = bf16[2048,256]{1,0:T(8,128)(2,1)S(1)} fusion(bf16[256,2048]{0,1:T(8,128)(2,1)S(1)} %copy.19, s32[2048]{0:T(1024)S(1)} %fusion.53), kind=kCustom, calls=%fused_computation.3.clone | custom fusion | bytes 2105344 | tf_op jit(solution)/shard_map/jit(_take)/gather | solution.py:65
  160.7 7.5 %gather_fusion.4 = bf16[2048,256]{1,0:T(8,128)(2,1)S(1)} fusion(bf16[256,2048]{0,1:T(8,128)(2,1)S(1)} %copy.18, s32[2048]{0:T(1024)S(1)} %fusion.53), kind=kCustom, calls=%fused_computation.2.clone | custom fusion | bytes 2105344 | tf_op jit(solution)/shard_map/jit(_take)/gather | solution.py:63
  168.3 0.7 convolution_bitcast_fusion.2
  168.9 0.6 fusion.10
  169.7 0.5 fusion.36
  170.2 0.3 copy-done.7
  170.6 0.1 copy-done.9
  170.8 3.2 %collective-permute-start = (f32[4,6,32,256]{3,2,0,1:T(8,128)S(1)}, f32[4,6,32,256]{3,2,0,1:T(8,128)S(1)}, u32[]{:S(2)}, u32[]{:S(2)}) collective-permute-start(f32[4,6,32,256]{3,2,0,1:T(8,128)S(1)} %pad_maximum_fusion), channel_id=1, source_target_pairs={{0,1},{1,0},{2,3},{3,2},{4,5},{5,4},{6,7},{7,6},{8,9},{9,8},{10,11... | collective-permute-start | bytes 2359304 | tf_op jit(solution)/shard_map/ppermute | solution.py:14
  174.0 17.7 %collective-permute-done = f32[4,6,32,256]{3,2,0,1:T(8,128)S(1)} collective-permute-done((f32[4,6,32,256]{3,2,0,1:T(8,128)S(1)}, f32[4,6,32,256]{3,2,0,1:T(8,128)S(1)}, u32[]{:S(2)}, u32[]{:S(2)}) %collective-permute-start) | collective-permute-done | bytes 786464 | tf_op jit(solution)/shard_map/ppermute | solution.py:14
  191.7 0.1 fusion.64
  191.8 4.2 %collective-permute-start.1 = (f32[4,6,32,256]{3,2,0,1:T(8,128)S(1)}, f32[4,6,32,256]{3,2,0,1:T(8,128)S(1)}, u32[]{:S(2)}, u32[]{:S(2)}) collective-permute-start(f32[4,6,32,256]{3,2,0,1:T(8,128)S(1)} %fusion.64), channel_id=1, source_target_pairs={{0,2},{1,3},{2,0},{3,1},{4,6},{5,7},{6,4},{7,5},{8,10},{9,11},{10,... | collective-permute-start | bytes 2359304 | tf_op jit(solution)/shard_map/ppermute | solution.py:14
  196.0 33.9 %collective-permute-done.1 = f32[4,6,32,256]{3,2,0,1:T(8,128)S(1)} collective-permute-done((f32[4,6,32,256]{3,2,0,1:T(8,128)S(1)}, f32[4,6,32,256]{3,2,0,1:T(8,128)S(1)}, u32[]{:S(2)}, u32[]{:S(2)}) %collective-permute-start.1) | collective-permute-done | bytes 786464 | tf_op jit(solution)/shard_map/ppermute | solution.py:14
  229.9 0.2 fusion.71
  230.1 8.6 %collective-permute-start.2 = (f32[4,6,32,256]{3,2,0,1:T(8,128)S(1)}, f32[4,6,32,256]{3,2,0,1:T(8,128)S(1)}, u32[]{:S(2)}, u32[]{:S(2)}) collective-permute-start(f32[4,6,32,256]{3,2,0,1:T(8,128)S(1)} %fusion.71), channel_id=1, source_target_pairs={{0,4},{1,5},{2,6},{3,7},{4,0},{5,1},{6,2},{7,3},{8,12},{9,13},{10,... | collective-permute-start | bytes 2359304 | tf_op jit(solution)/shard_map/ppermute | solution.py:14
  238.7 34.1 %collective-permute-done.2 = f32[4,6,32,256]{3,2,0,1:T(8,128)S(1)} collective-permute-done((f32[4,6,32,256]{3,2,0,1:T(8,128)S(1)}, f32[4,6,32,256]{3,2,0,1:T(8,128)S(1)}, u32[]{:S(2)}, u32[]{:S(2)}) %collective-permute-start.2) | collective-permute-done | bytes 786464 | tf_op jit(solution)/shard_map/ppermute | solution.py:14
  272.9 0.6 fusion.50
  273.5 0.5 squeeze.45
  274.1 0.5 mul.158
  274.6 0.5 squeeze.42
  275.2 0.5 squeeze.44
  275.7 0.5 mul.154
  276.3 0.5 mul.152
  276.8 1.3 squeeze.43
  278.2 1.4 multiply_bitcast_fusion
  279.6 0.3 copy.26
  279.9 24.5 %all_to_all.22 = f32[4,64,1,4,4]{3,4,0,2,1:T(4,128)S(1)} all-to-all(f32[4,64,1,4,4]{3,4,0,2,1:T(4,128)S(1)} %copy.26), channel_id=1, replica_groups=mesh['dp'=64,'refl'=8] {'dp'}, dimensions={1} | all-to-all | bytes 32768 | tf_op jit(solution)/shard_map/all_to_all | solution.py:77
  304.4 0.9 copy.27
  (50 shorter events, 0.4 us)
Async XLA Ops:
  6.0 15.0 %copy-start = (bf16[32,2048]{1,0:T(8,128)(2,1)S(1)}, bf16[32,2048]{1,0:T(8,128)(2,1)}, u32[]{:S(2)}) copy-start(bf16[32,2048]{1,0:T(8,128)(2,1)} %param.7) | copy-start | bytes 393220
  6.0 15.0 %copy-start.5 = (s32[32,2048]{1,0:T(8,128)S(1)}, s32[32,2048]{1,0:T(8,128)}, u32[]{:S(2)}) copy-start(s32[32,2048]{1,0:T(8,128)} %param.8) | copy-start | bytes 786436
  6.0 15.0 %copy-start.6 = (bf16[32,2048]{1,0:T(8,128)(2,1)S(1)}, bf16[32,2048]{1,0:T(8,128)(2,1)}, u32[]{:S(2)}) copy-start(bf16[32,2048]{1,0:T(8,128)(2,1)} %param.9) | copy-start | bytes 393220
  6.0 43.5 %all-to-all-start.1 = ((bf16[64,4,2048]{2,1,0:T(4,128)(2,1)}), bf16[64,4,2048]{2,1,0:T(4,128)(2,1)S(1)}, u32[]{:S(2)}, u32[]{:S(2)}) async-start(bf16[64,4,2048]{2,1,0:T(4,128)(2,1)} %reshape.180), calls=%async_computation.1 | async-start | bytes 2097152 | tf_op jit(solution)/shard_map/all_to_all | solution.py:55
  22.4 1.2 copy-start.16
  49.5 34.7 %all-to-all-start = ((bf16[64,4,2048]{2,1,0:T(4,128)(2,1)}), bf16[64,4,2048]{2,1,0:T(4,128)(2,1)S(1)}, u32[]{:S(2)}, u32[]{:S(2)}) async-start(bf16[64,4,2048]{2,1,0:T(4,128)(2,1)} %reshape.172), calls=%async_computation | async-start | bytes 2097152 | tf_op jit(solution)/shard_map/all_to_all | solution.py:56
  122.7 2.6 copy-start.2
  122.7 2.6 copy-start.20
  125.3 1.3 copy-start.1
  125.3 1.5 copy-start.3
  125.3 1.5 copy-start.19
  148.2 2.6 copy-start.4
  148.2 2.6 copy-start.18
  160.7 7.5 %copy-start.17 = (pred[2048]{0:T(1024)(128)(4,1)S(1)}, pred[2048]{0:T(1024)(128)(4,1)}, u32[]{:S(2)}) copy-start(pred[2048]{0:T(1024)(128)(4,1)} %compare_and_fusion.2) | copy-start | bytes 6148
  169.6 0.9 copy-start.7
  169.6 0.9 copy-start.8
  169.6 0.9 copy-start.10
  169.6 0.9 copy-start.11
  169.6 0.9 copy-start.13
  169.6 0.9 copy-start.14
  169.6 1.0 copy-start.9
  169.6 1.0 copy-start.12
  169.6 1.0 copy-start.15
  170.8 20.9 %collective-permute-start = (f32[4,6,32,256]{3,2,0,1:T(8,128)S(1)}, f32[4,6,32,256]{3,2,0,1:T(8,128)S(1)}, u32[]{:S(2)}, u32[]{:S(2)}) collective-permute-start(f32[4,6,32,256]{3,2,0,1:T(8,128)S(1)} %pad_maximum_fusion), channel_id=1, source_target_pairs={{0,1},{1,0},{2,3},{3,2},{4,5},{5,4},{6,7},{7,6},{8,9},{9,8},{10,11... | collective-permute-start | bytes 2359304 | tf_op jit(solution)/shard_map/ppermute | solution.py:14
  191.8 38.1 %collective-permute-start.1 = (f32[4,6,32,256]{3,2,0,1:T(8,128)S(1)}, f32[4,6,32,256]{3,2,0,1:T(8,128)S(1)}, u32[]{:S(2)}, u32[]{:S(2)}) collective-permute-start(f32[4,6,32,256]{3,2,0,1:T(8,128)S(1)} %fusion.64), channel_id=1, source_target_pairs={{0,2},{1,3},{2,0},{3,1},{4,6},{5,7},{6,4},{7,5},{8,10},{9,11},{10,... | collective-permute-start | bytes 2359304 | tf_op jit(solution)/shard_map/ppermute | solution.py:14
  230.1 42.7 %collective-permute-start.2 = (f32[4,6,32,256]{3,2,0,1:T(8,128)S(1)}, f32[4,6,32,256]{3,2,0,1:T(8,128)S(1)}, u32[]{:S(2)}, u32[]{:S(2)}) collective-permute-start(f32[4,6,32,256]{3,2,0,1:T(8,128)S(1)} %fusion.71), channel_id=1, source_target_pairs={{0,4},{1,5},{2,6},{3,7},{4,0},{5,1},{6,2},{7,3},{8,12},{9,13},{10,... | collective-permute-start | bytes 2359304 | tf_op jit(solution)/shard_map/ppermute | solution.py:14
